TPU v7x, 128 devices: a whole 4x4x4 slice. The times are simulated.
128 devices in a mesh: dp: 16 (over y, z), ctx: 8 (over x, core).
Axes of the slice: x: 4, y: 4, z: 4, core: 2. Of those that a mesh axis runs over, the one named last changes fastest.
Arguments:
- state_input: bfloat16 [32768, 4096], P(('dp', 'ctx')), may hold values from -6 to 6
- gate_values: bfloat16 [32768, 4096], P(('dp', 'ctx')), may hold values from -6 to 6
- input_matrix: bfloat16 [32768, 512], P(('dp', 'ctx')), may hold values from -1.2 to 1.2
- readout_matrix: bfloat16 [32768, 512], P(('dp', 'ctx')), may hold values from -1.1953125 to 1.1953125
- step_unbiased: float32 [32768, 64], P(('dp', 'ctx')), may hold values from -3 to 2560
- step_bias: float32 [64], replicated, may hold values from -1 to 0.5
- decay_rate_log: float32 [64], replicated
- skip_coefficients: float32 [64], replicated, may hold values from 3 to 10
- norm_gain: float32 [4096], replicated, may hold values from 0.1 to 8
- adapter_down: bfloat16 [64, 4096], replicated, may hold values from -0.09375 to 0.09375
- adapter_up: bfloat16 [64, 2048], replicated, may hold values from -0.75 to 0.75
- projection_weight: bfloat16 [2048, 4096], P(('dp', 'ctx')), may hold values from -0.09375 to 0.09375
- output_cotangent: bfloat16 [32768, 2048], P(('dp', 'ctx')), may hold values from -30 to 30
Outputs:
- input_gradient: bfloat16 [32768, 4096], P(('dp', 'ctx'))
- adapter_down_gradient: float32 [64, 4096], P(None, ('dp', 'ctx'))
- adapter_up_gradient: float32 [64, 2048], P(None, ('dp', 'ctx'))
All inputs are finite; a program needn't handle non-finite values.
Results may differ from a plain program's by a relative error of at most 0.009.
Values may be sent and summed in bfloat16 or wider, within the bound.
A program may use at most 192 MiB of HBM per device.

v0:
```python
import jax
import jax.numpy as jnp
from jax import lax
from jax.sharding import PartitionSpec as P

H = 64
P_SIZE = 64
N = 128
G = 4
Q = 256
INNER_CHANNELS = 4096
EPS_NORM = 1e-05
CLIP_EPSILON = 1e-06
ADAPTER_SCALE = 2.0


def entering(value, axis, join, neutral):
    count, mine = (lax.axis_size(axis), lax.axis_index(axis))
    pieces = jax.tree.map(lambda part: lax.all_gather(part, axis), value)
    running = jax.tree.map(
        lambda part, zero: jnp.full_like(part, 0) + jnp.asarray(zero, part.dtype), value, neutral
    )

    def lap(position, running):
        longer = join(running, jax.tree.map(lambda part: part[position], pieces))
        return jax.tree.map(lambda new, old: jnp.where(position < mine, new, old), longer, running)

    return lax.fori_loop(0, count - 1, lap, running)


def carried_in(value, axis, join, neutral):
    count = lax.axis_size(axis)
    place = lax.axis_index(axis)
    ahead = count - 1 - place
    gathered = jax.tree.map(
        lambda a, kind: lax.all_gather(a.astype(kind), axis), value, (jnp.bfloat16, jnp.bfloat16)
    )
    state = jax.tree.map(lambda a, e: jnp.zeros_like(a) + jnp.asarray(e, a.dtype), value, neutral)

    def one(lap, state):
        source = count - 1 - lap
        return join(
            state,
            jax.tree.map(
                lambda a, own: lax.dynamic_index_in_dim(a, source, 0, False).astype(own.dtype),
                gathered,
                value,
            ),
        )

    return lax.fori_loop(0, ahead, one, state)


def combine(earlier, later):
    return (earlier[0] * later[0], earlier[1] * later[0][:, None, None] + later[1])


def spread_heads(grouped, lead):
    wide = jnp.broadcast_to(grouped[..., :, None, :], lead + (G, H // G, grouped.shape[-1]))
    return wide.reshape(lead + (H, grouped.shape[-1]))


def on_device(
    state_input,
    gate_values,
    input_matrix,
    readout_matrix,
    step_unbiased,
    step_bias,
    decay_rate_log,
    skip_coefficients,
    norm_gain,
    adapter_down,
    adapter_up,
    projection_weight,
    output_cotangent,
):
    row_count = state_input.shape[0]
    block_count = row_count // Q
    group_width = INNER_CHANNELS // G
    per_group = H // G
    step_size = jax.nn.softplus(step_unbiased + step_bias[None, :])
    cum_decay = jnp.cumsum(
        (-jnp.exp(decay_rate_log)[None, :] * step_size).reshape(block_count, Q, H), axis=1
    )
    block_total = cum_decay[:, -1, :]
    x_heads = state_input.reshape(row_count, H, P_SIZE)
    xdt_all = (
        (x_heads * step_size[:, :, None]).astype(jnp.bfloat16).reshape(block_count, Q, H, P_SIZE)
    )
    b_blocks = input_matrix.reshape(block_count, Q, G, N)
    c_blocks = readout_matrix.reshape(block_count, Q, G, N)
    inner_prod = jnp.einsum(
        "kign,kjgn->kgij", c_blocks, b_blocks, preferred_element_type=jnp.float32
    )
    inner_prod = jnp.broadcast_to(
        inner_prod[:, :, None], (block_count, G, per_group, Q, Q)
    ).reshape(block_count, H, Q, Q)
    cum_heads = jnp.swapaxes(cum_decay, 1, 2)
    gap_logs = cum_heads[:, :, :, None] - cum_heads[:, :, None, :]
    causal = (
        lax.broadcasted_iota(jnp.int32, (Q, Q), 0) >= lax.broadcasted_iota(jnp.int32, (Q, Q), 1)
    )[None, None]
    scores = (
        inner_prod * jnp.where(causal, jnp.exp(jnp.where(causal, gap_logs, 0.0)), 0.0)
    ).astype(jnp.bfloat16)
    intra_part = jnp.einsum("khij,kjhp->kihp", scores, xdt_all, preferred_element_type=jnp.float32)
    b_heads = spread_heads(b_blocks, (block_count, Q))
    b_weighted = (jnp.exp(block_total[:, None, :] - cum_decay)[..., None] * b_heads).astype(
        jnp.bfloat16
    )
    block_state = jnp.einsum(
        "kjhn,kjhp->khnp", b_weighted, xdt_all, preferred_element_type=jnp.float32
    )

    def step_forward(run_state, block_item):
        decay_log, fresh_state = block_item
        return (jnp.exp(decay_log)[:, None, None] * run_state + fresh_state, run_state)

    zero_state = jnp.zeros((H, N, P_SIZE), jnp.float32)
    device_state, local_in = lax.scan(step_forward, zero_state, (block_total, block_state))
    device_decay = jnp.exp(jnp.sum(block_total, axis=0))
    identity = (jnp.ones((H,), jnp.float32), zero_state)
    unused_decay, incoming = entering((device_decay, device_state), "ctx", combine, identity)
    before = jnp.cumsum(block_total, axis=0) - block_total
    state_in = local_in + jnp.exp(before)[:, :, None, None] * incoming[None]
    incoming_bf = state_in.astype(jnp.bfloat16).reshape(block_count, G, per_group, N, P_SIZE)
    inter_part = jnp.einsum(
        "kign,kgmnp->kigmp", c_blocks, incoming_bf, preferred_element_type=jnp.float32
    ).reshape(block_count, Q, H, P_SIZE)
    ssd_heads = (intra_part + jnp.exp(cum_decay)[..., None] * inter_part).reshape(
        row_count, H, P_SIZE
    ) + skip_coefficients[None, :, None] * x_heads
    silu_z = jax.nn.silu(gate_values.astype(jnp.float32))
    weight_groups = norm_gain.reshape(G, group_width)
    gated = (ssd_heads.reshape(row_count, INNER_CHANNELS) * silu_z).reshape(
        row_count, G, group_width
    )
    rstd = lax.rsqrt(jnp.mean(gated * gated, axis=-1, keepdims=True) + EPS_NORM)
    normalized = (
        (gated * rstd * weight_groups).reshape(row_count, INNER_CHANNELS).astype(jnp.bfloat16)
    )
    down_product = lax.dot_general(
        normalized, adapter_down, (((1,), (1,)), ((), ())), preferred_element_type=jnp.float32
    ).astype(jnp.bfloat16)
    upper_gradient = lax.dot_general(
        output_cotangent, adapter_up, (((1,), (1,)), ((), ())), preferred_element_type=jnp.float32
    ).astype(jnp.bfloat16)
    down_portion = ADAPTER_SCALE * lax.dot_general(
        upper_gradient, normalized, (((0,), (0,)), ((), ())), preferred_element_type=jnp.float32
    )
    up_portion = ADAPTER_SCALE * lax.dot_general(
        down_product, output_cotangent, (((0,), (0,)), ((), ())), preferred_element_type=jnp.float32
    )
    adapter_initial = ADAPTER_SCALE * jnp.dot(
        upper_gradient, adapter_down, preferred_element_type=jnp.float32
    )
    combined_weight = lax.all_gather(projection_weight, ("dp", "ctx"), axis=0, tiled=True)
    normed_gradient = adapter_initial + jnp.dot(
        output_cotangent, combined_weight, preferred_element_type=jnp.float32
    )
    weighted_grad = normed_gradient.reshape(row_count, G, group_width) * weight_groups
    d_gated = rstd * weighted_grad - gated * (rstd * rstd * rstd) * jnp.mean(
        gated * weighted_grad, axis=-1, keepdims=True
    )
    d_ssd = d_gated.reshape(row_count, INNER_CHANNELS) * silu_z
    d_ssd_bf = d_ssd.reshape(block_count, Q, H, P_SIZE).astype(jnp.bfloat16)
    intra_back = jnp.einsum("khij,kihp->kjhp", scores, d_ssd_bf, preferred_element_type=jnp.float32)
    c_heads = spread_heads(c_blocks, (block_count, Q))
    c_weighted = (jnp.exp(cum_decay)[..., None] * c_heads).astype(jnp.bfloat16)
    block_grad = jnp.einsum(
        "kihn,kihp->khnp", c_weighted, d_ssd_bf, preferred_element_type=jnp.float32
    )

    def step_backward(grad_state, block_item):
        decay_log, fresh_state = block_item
        return (jnp.exp(decay_log)[:, None, None] * grad_state + fresh_state, grad_state)

    device_grad, local_out = lax.scan(
        step_backward, zero_state, (block_total, block_grad), reverse=True
    )
    unused_back, outgoing = carried_in((device_decay, device_grad), "ctx", combine, identity)
    after_sum = jnp.flip(jnp.cumsum(jnp.flip(block_total, axis=0), axis=0), axis=0) - block_total
    grad_in = local_out + jnp.exp(after_sum)[:, :, None, None] * outgoing[None]
    outgoing_bf = grad_in.astype(jnp.bfloat16)
    cross_part = jnp.einsum(
        "kjhn,khnp->kjhp", b_weighted, outgoing_bf, preferred_element_type=jnp.float32
    )
    grad_heads = step_size[:, :, None] * (intra_back + cross_part).reshape(
        row_count, H, P_SIZE
    ) + skip_coefficients[None, :, None] * d_ssd.reshape(row_count, H, P_SIZE)
    input_gradient = grad_heads.reshape(row_count, INNER_CHANNELS).astype(jnp.bfloat16)
    down_total, up_total = lax.psum((down_portion, up_portion), ("dp", "ctx"))
    down_root_mean = jnp.sqrt(jnp.mean(down_total * down_total) + CLIP_EPSILON)
    up_root_mean = jnp.sqrt(jnp.mean(up_total * up_total) + CLIP_EPSILON)
    device_total = lax.axis_size(("dp", "ctx"))
    position = lax.axis_index(("dp", "ctx"))
    width_a = down_total.shape[1] // device_total
    width_b = up_total.shape[1] // device_total
    down_fraction = lax.dynamic_slice_in_dim(down_total, position * width_a, width_a, 1)
    up_fraction = lax.dynamic_slice_in_dim(up_total, position * width_b, width_b, 1)
    adapter_down_gradient = down_fraction / jnp.maximum(1.0, down_root_mean)
    adapter_up_gradient = up_fraction / jnp.maximum(1.0, up_root_mean)
    return (input_gradient, adapter_down_gradient, adapter_up_gradient)


def solution(mesh):
    placed = (
        P(("dp", "ctx"), None),
        P(("dp", "ctx"), None),
        P(("dp", "ctx"), None),
        P(("dp", "ctx"), None),
        P(("dp", "ctx"), None),
        P(),
        P(),
        P(),
        P(),
        P(),
        P(),
        P(("dp", "ctx"), None),
        P(("dp", "ctx"), None),
    )
    return jax.shard_map(
        on_device,
        mesh=mesh,
        in_specs=placed,
        out_specs=(P(("dp", "ctx"), None), P(None, ("dp", "ctx")), P(None, ("dp", "ctx"))),
        check_vma=False,
    )
```

profile of v0, /device:TPU:0, one launch (start us, length us, event | category | flops | bytes accessed | tf_op | source)
XLA Modules:
  0.0 570.3 jit_solution(756266060873161029)
XLA Ops:
  14.8 3.0 copy.131
  17.7 3.8 fusion.3
  28.1 5.6 fusion.1
  33.8 11.3 %all-gather = f32[8,1,64]{2,1,0:T(1,128)} all-gather(f32[1,1,64]{2,1,0:T(1,128)S(1)} %copy-done.22), channel_id=2, replica_groups=mesh['dp'=16,'ctx'=8] {'ctx'}, dimensions={0}, use_global_device_ids=true | all-gather | bytes 2304 | tf_op jit(solution)/shard_map/all_gather | solution.py:19
  46.1 67.2 %all-gather.10.cloned.1.call-done = f32[512,128,64]{1,2,0:T(8,128)} async-done(((f32[64,128,64]{1,2,0:T(8,128)}), f32[512,128,64]{1,2,0:T(8,128)}) %all-gather.10.cloned.1.call-update) | async-done | bytes 16777232 | tf_op jit(solution)/shard_map/all_gather | solution.py:19
  113.3 80.0 %while.19 = (s32[]{:T(128)}, f32[64,128,64]{2,1,0:T(8,128)}, s32[]{:T(128)}, f32[8,64]{1,0:T(8,128)}, f32[8,64,128,64]{2,3,1,0:T(8,128)}, /*index=5*/s32[]{:T(128)}, s32[]{:T(128)}) while((s32[]{:T(128)}, f32[64,128,64]{2,1,0:T(8,128)}, s32[]{:T(128)}, f32[8,64]{1,0:T(8,128)}, f32[8,64,128,64]{2,3,1,0:T(8,128)}, ...), condition=%wide.region_3.4_spmd.clone, body=%wide.region_2.3_spmd.clone.sunk | while | flops 2097156 | bytes 14680945 | solution.py:28
  115.0 2.8 copy.195
  118.5 4.9 fusion.43
  125.1 2.8 copy.195
  128.6 6.1 %fusion.43 = f32[64,128,64]{2,1,0:T(8,128)} fusion(f32[1,64,128,64]{3,2,1,0:T(8,128)} %copy.195, f32[64,128,64]{2,1,0:T(8,128)} %get-tuple-element.418, f32[64]{0:T(128)S(1)} %dynamic-slice_bitcast_fusion.2, pred[]{:T(512)S(6)} %compare.3, pred[]{:T(512)S(6)} %lt.51), kind=kLoop, calls=%fused_computation.4.clone.1 | loop fusion | flops 2097152 | bytes 6291714 | tf_op jit(solution)/shard_map/while/body/eval_jaxpr/jit(_where)/select_n | solution.py:26
  136.4 2.8 copy.195
  139.9 6.1 %fusion.43 = f32[64,128,64]{2,1,0:T(8,128)} fusion(f32[1,64,128,64]{3,2,1,0:T(8,128)} %copy.195, f32[64,128,64]{2,1,0:T(8,128)} %get-tuple-element.418, f32[64]{0:T(128)S(1)} %dynamic-slice_bitcast_fusion.2, pred[]{:T(512)S(6)} %compare.3, pred[]{:T(512)S(6)} %lt.51), kind=kLoop, calls=%fused_computation.4.clone.1 | loop fusion | flops 2097152 | bytes 6291714 | tf_op jit(solution)/shard_map/while/body/eval_jaxpr/jit(_where)/select_n | solution.py:26
  147.8 2.8 copy.195
  151.2 6.3 %fusion.43 = f32[64,128,64]{2,1,0:T(8,128)} fusion(f32[1,64,128,64]{3,2,1,0:T(8,128)} %copy.195, f32[64,128,64]{2,1,0:T(8,128)} %get-tuple-element.418, f32[64]{0:T(128)S(1)} %dynamic-slice_bitcast_fusion.2, pred[]{:T(512)S(6)} %compare.3, pred[]{:T(512)S(6)} %lt.51), kind=kLoop, calls=%fused_computation.4.clone.1 | loop fusion | flops 2097152 | bytes 6291714 | tf_op jit(solution)/shard_map/while/body/eval_jaxpr/jit(_where)/select_n | solution.py:26
  159.3 2.8 copy.195
  162.8 6.1 %fusion.43 = f32[64,128,64]{2,1,0:T(8,128)} fusion(f32[1,64,128,64]{3,2,1,0:T(8,128)} %copy.195, f32[64,128,64]{2,1,0:T(8,128)} %get-tuple-element.418, f32[64]{0:T(128)S(1)} %dynamic-slice_bitcast_fusion.2, pred[]{:T(512)S(6)} %compare.3, pred[]{:T(512)S(6)} %lt.51), kind=kLoop, calls=%fused_computation.4.clone.1 | loop fusion | flops 2097152 | bytes 6291714 | tf_op jit(solution)/shard_map/while/body/eval_jaxpr/jit(_where)/select_n | solution.py:26
  168.9 2.4 constant_dynamic-slice_fusion.5
  171.3 2.8 copy.195
  174.7 6.8 %fusion.43 = f32[64,128,64]{2,1,0:T(8,128)} fusion(f32[1,64,128,64]{3,2,1,0:T(8,128)} %copy.195, f32[64,128,64]{2,1,0:T(8,128)} %get-tuple-element.418, f32[64]{0:T(128)S(1)} %dynamic-slice_bitcast_fusion.2, pred[]{:T(512)S(6)} %compare.3, pred[]{:T(512)S(6)} %lt.51), kind=kLoop, calls=%fused_computation.4.clone.1 | loop fusion | flops 2097152 | bytes 6291714 | tf_op jit(solution)/shard_map/while/body/eval_jaxpr/jit(_where)/select_n | solution.py:26
  183.3 2.8 copy.195
  186.8 6.5 %fusion.43 = f32[64,128,64]{2,1,0:T(8,128)} fusion(f32[1,64,128,64]{3,2,1,0:T(8,128)} %copy.195, f32[64,128,64]{2,1,0:T(8,128)} %get-tuple-element.418, f32[64]{0:T(128)S(1)} %dynamic-slice_bitcast_fusion.2, pred[]{:T(512)S(6)} %compare.3, pred[]{:T(512)S(6)} %lt.51), kind=kLoop, calls=%fused_computation.4.clone.1 | loop fusion | flops 2097152 | bytes 6291714 | tf_op jit(solution)/shard_map/while/body/eval_jaxpr/jit(_where)/select_n | solution.py:26
  193.4 2.9 multiply_convert_fusion.2
  196.3 2.9 fusion.15
  199.2 8.2 %fusion.8 = f32[1,256,64,64]{1,3,2,0:T(8,128)} fusion(f32[4,16,64,256]{3,2,1,0:T(8,128)} %fusion.15, bf16[64,256,256]{2,1,0:T(8,128)(2,1)S(1)} %copy-done.1, f32[256,64]{0,1:T(8,128)S(1)} %copy.139, f32[256,64,64]{0,2,1:T(8,128)} %bitcast.133, f32[256,64]{0,1:T(8,128)S(1)} %get-tuple-element.338), kind=kOutput, calls=%fused_computation.22 | convolution fusion | flops 541065216 | bytes 21102592 | tf_op jit(solution)/shard_map/khij,kjhp->kihp/dot_general | solution.py:107
  207.3 5.8 %copy.145 = f32[256,4096]{1,0:T(8,128)} copy(f32[256,4096]{0,1:T(8,128)} %bitcast.141) | data formatting | bytes 8388608 | tf_op jit(solution)/shard_map/reshape | solution.py:131
  213.1 6.2 %add_multiply_fusion = f32[256,4096]{1,0:T(8,128)} fusion(f32[256,4096]{1,0:T(8,128)} %copy.145, f32[4096]{0:T(1024)S(1)} %mul.324, bf16[256,4096]{1,0:T(8,128)(2,1)} %param.18, bf16[256,4096]{1,0:T(8,128)(2,1)S(1)} %copy-done.8), kind=kLoop, calls=%fused_computation.29 | loop fusion | flops 9437184 | bytes 12599296 | tf_op jit(solution)/shard_map/mul | solution.py:136
  219.4 6.0 %reshape.335 = f32[256,4,1024]{2,1,0:T(4,128)} reshape(f32[256,4096]{1,0:T(8,128)} %add_multiply_fusion) | data formatting | bytes 8388608 | tf_op jit(solution)/shard_map/reshape | solution.py:136
  225.4 8.2 %fusion.19 = f32[256,4096]{1,0:T(8,128)S(1)} fusion(bf16[256,2048]{1,0:T(8,128)(2,1)S(1)} %copy-done, bf16[2048,4096]{1,0:T(8,128)(2,1)} %all-gather.8.cloned.1.call-done), kind=kOutput, calls=%fused_computation.71 | convolution fusion | flops 4294967296 | bytes 22020096 | tf_op jit(solution)/shard_map/dot_general | solution.py:159
  233.6 2.7 fusion.4
  236.3 6.0 %reshape.336 = f32[256,4,1024]{2,1,0:T(4,128)} reshape(f32[256,4096]{1,0:T(8,128)} %fusion.4) | data formatting | bytes 8388608 | tf_op jit(solution)/shard_map/reshape | solution.py:162
  242.3 4.8 multiply_reduce_fusion.1
  247.7 5.8 %copy.175 = f32[32,8,4,1024]{3,1,2,0:T(8,128)} copy(f32[32,8,4,1024]{3,2,1,0:T(4,128)S(1)} %bitcast.142) | data formatting | bytes 8388608
  254.4 5.8 %copy.174 = f32[32,8,4,1024]{3,1,2,0:T(8,128)} copy(f32[32,8,4,1024]{3,2,1,0:T(4,128)S(1)} %bitcast.143) | data formatting | bytes 8388608
  261.0 4.2 copy.173
  265.2 6.4 %fusion.18 = (bf16[256,4096]{1,0:T(8,128)(2,1)}, f32[256,4096]{1,0:T(8,128)}, bf16[256,4096]{1,0:T(8,128)(2,1)S(1)}) fusion(bf16[256,4096]{1,0:T(8,128)(2,1)} %param.18, f32[256,4096]{1,0:T(8,128)S(1)} %bitcast.137, f32[256,4096]{1,0:T(8,128)S(1)} %copy-done.4, f32[256,4096]{1,0:T(8,128)} %bitcast.138, f32[256,4096]{1,0:T(8,128)S(1)} %bitcast.139, ...), kind=kLoop, calls=%fused_computation.70 | loop fusion | flops 15728640 | bytes 31473664 | tf_op jit(solution)/shard_map/convert_element_type | solution.py:167
  273.0 3.1 convolution_multiply_fusion.2
  276.3 3.8 fusion.2
  280.1 3.3 copy.151
  283.4 4.2 add_convert_fusion.1
  287.6 2.3 mul.307
  289.9 5.7 copy.156
  295.6 9.0 %all-gather.3 = bf16[8,1,64]{2,1,0:T(2,128)(2,1)S(1)} all-gather(bf16[1,1,64]{2,1,0:T(2,128)(2,1)S(1)} %copy-done.21), channel_id=5, replica_groups=mesh['dp'=16,'ctx'=8] {'ctx'}, dimensions={0}, use_global_device_ids=true | all-gather | bytes 1152 | tf_op jit(solution)/shard_map/all_gather | solution.py:36
  304.5 7.0 %fusion.20 = f32[64,64,256]{2,1,0:T(8,128)} fusion(bf16[256,64,64]{0,2,1:T(8,128)(2,1)S(1)} %bitcast.136, bf16[64,256,256]{2,1,0:T(8,128)(2,1)} %fusion.1), kind=kOutput, calls=%fused_computation.72 | convolution fusion | flops 536870912 | bytes 14680064 | tf_op jit(solution)/shard_map/khij,kihp->kjhp/dot_general | solution.py:168
  311.5 115.6 %all-reduce.3.cloned.1.call-done = (f32[64,4096]{1,0:T(8,128)}, f32[64,2048]{1,0:T(8,128)}) async-done(((f32[64,4096]{1,0:T(8,128)}, f32[64,2048]{1,0:T(8,128)}), (f32[64,4096]{1,0:T(8,128)}, f32[64,2048]{1,0:T(8,128)})) %all-reduce.3.cloned.1.call-update) | async-done | bytes 1572880 | tf_op jit(solution)/shard_map/psum | solution.py:193
  435.4 41.6 %all-gather.12.cloned.1.call-done = bf16[512,128,64]{1,2,0:T(8,128)(2,1)} async-done(((bf16[64,128,64]{1,2,0:T(8,128)(2,1)}), bf16[512,128,64]{1,2,0:T(8,128)(2,1)}) %all-gather.12.cloned.1.call-update) | async-done | bytes 8388624 | tf_op jit(solution)/shard_map/all_gather | solution.py:36
  476.9 2.5 broadcast_in_dim.45
  479.5 62.9 %while.18 = (s32[]{:T(128)}, f32[64,128,64]{2,1,0:T(8,128)}, s32[]{:T(128)}, bf16[8,64]{1,0:T(8,128)(2,1)S(1)}, bf16[8,64,128,64]{2,3,1,0:T(8,128)(2,1)}, /*index=5*/s32[]{:T(128)}, s32[]{:T(128)}, s32[]{:T(128)}, s32[]{:T(128)}) while((s32[]{:T(128)}, f32[64,128,64]{2,1,0:T(8,128)}, s32[]{:T(128)}, bf16[8,64]{1,0:T(8,128)(2,1)S(1)}, ...), condition=%wide.region_7.8_spmd, body=%wide.region_6.7_spmd.sunk | while | flops 1572934 | bytes 9437979 | solution.py:51
  479.5 2.3 constant_dynamic-slice_fusion.4
  483.8 4.7 convert_add_fusion.2
  488.5 2.3 constant_dynamic-slice_fusion.4
  492.8 4.7 convert_add_fusion.2
  497.4 2.3 constant_dynamic-slice_fusion.4
  501.8 4.7 convert_add_fusion.2
  506.4 2.3 constant_dynamic-slice_fusion.4
  510.7 4.7 convert_add_fusion.2
  515.4 2.3 constant_dynamic-slice_fusion.4
  519.7 4.7 convert_add_fusion.2
  524.4 2.3 constant_dynamic-slice_fusion.4
  528.7 4.7 convert_add_fusion.2
  533.4 2.3 constant_dynamic-slice_fusion.4
  537.7 4.7 convert_add_fusion.2
  542.4 8.3 %convolution_add_fusion = f32[64,64,256]{2,1,0:T(8,128)} fusion(f32[64,64,256]{2,1,0:T(8,128)} %fusion.20, bf16[256,64,128]{2,0,1:T(8,128)(2,1)} %copy-done.2, f32[64,128,64]{2,1,0:T(8,128)} %get-tuple-element.212, f32[64]{0:T(128)S(1)} %copy-done.20), kind=kOutput, calls=%fused_computation.33 | convolution fusion | flops 270532608 | bytes 14680320 | tf_op jit(solution)/shard_map/kjhn,khnp->kjhp/dot_general | solution.py:186
  550.7 5.6 copy.157
  556.3 7.3 %add_convert_fusion = bf16[256,4096]{1,0:T(8,128)(2,1)} fusion(f32[256,4096]{1,0:T(8,128)} %get-tuple-element.334, f32[256,4096]{1,0:T(8,128)} %copy.156, f32[256,4096]{1,0:T(8,128)} %copy.157, f32[4096]{0:T(1024)S(1)} %mul.324), kind=kLoop, calls=%fused_computation.24 | loop fusion | flops 4194304 | bytes 14696448 | tf_op jit(solution)/shard_map/convert_element_type | solution.py:192
  (135 shorter events, 55.2 us)
Async XLA Ops:
  7.2 37.9 %copy-start = (bf16[256,2048]{1,0:T(8,128)(2,1)S(1)}, bf16[256,2048]{1,0:T(8,128)(2,1)}, u32[]{:S(2)}) copy-start(bf16[256,2048]{1,0:T(8,128)(2,1)} %param.29) | copy-start | bytes 3145732
  7.2 7.6 %copy-start.7 = (bf16[256,4096]{1,0:T(8,128)(2,1)S(1)}, bf16[256,4096]{1,0:T(8,128)(2,1)}, u32[]{:S(2)}) copy-start(bf16[256,4096]{1,0:T(8,128)(2,1)} %param.17) | copy-start | bytes 6291460
  7.2 106.1 %all-gather.10.cloned.1.call-start = ((), (), s32[]{:S(2)}) async-start(), calls=%async_computation.1 | async-start | bytes 18874368 | tf_op jit(solution)/shard_map/all_gather | solution.py:19
  10.7 0.6 copy-start.12
  11.9 9.7 %copy-start.23 = (f32[64]{0:T(128)}, f32[64]{0:T(128)S(1)}, u32[]{:S(2)}) copy-start(f32[64]{0:T(128)S(1)} %get-tuple-element.344) | copy-start | bytes 772
  17.7 5.8 %copy-start.3 = (f32[256,4096]{0,1:T(8,128)S(1)}, f32[256,4096]{0,1:T(8,128)}, u32[]{:S(2)}) copy-start(f32[256,4096]{0,1:T(8,128)} %copy.131) | copy-start | bytes 12582916
  21.6 1.9 copy-start.2
  23.5 3.2 copy-start.11
  23.5 3.3 copy-start.13
  23.5 3.4 copy-start.25
  23.5 3.6 copy-start.17
  23.5 4.2 copy-start.10
  25.8 199.6 %all-gather.8.cloned.1.call-start = ((), (), s32[]{:S(2)}) async-start(), calls=%async_computation | async-start | bytes 16908288 | tf_op jit(solution)/shard_map/all_gather | solution.py:158
  26.6 400.5 %all-reduce.3.cloned.1.call-start = ((), (), s32[]{:S(2)}) async-start(), calls=%async_computation.3 | async-start | bytes 3145728 | tf_op jit(solution)/shard_map/psum | solution.py:193
  28.1 5.7 copy-start.22
  28.1 16.9 %copy-start.16 = (bf16[64,2048]{1,0:T(8,128)(2,1)S(1)}, bf16[64,2048]{1,0:T(8,128)(2,1)}, u32[]{:S(2)}) copy-start(bf16[64,2048]{1,0:T(8,128)(2,1)} %param.27) | copy-start | bytes 786436
  193.4 5.8 %copy-start.1 = (bf16[64,256,256]{2,1,0:T(8,128)(2,1)S(1)}, bf16[64,256,256]{2,1,0:T(8,128)(2,1)}, u32[]{:S(2)}) copy-start(bf16[64,256,256]{2,1,0:T(8,128)(2,1)} %fusion.1) | copy-start | bytes 25165828
  207.3 5.8 %copy-start.8 = (bf16[256,4096]{1,0:T(8,128)(2,1)S(1)}, bf16[256,4096]{1,0:T(8,128)(2,1)}, u32[]{:S(2)}) copy-start(bf16[256,4096]{1,0:T(8,128)(2,1)} %param.17) | copy-start | bytes 6291460
  225.4 8.2 %copy-start.9 = (bf16[64,4096]{1,0:T(8,128)(2,1)S(1)}, bf16[64,4096]{1,0:T(8,128)(2,1)}, u32[]{:S(2)}) copy-start(bf16[64,4096]{1,0:T(8,128)(2,1)} %param.26) | copy-start | bytes 1572868
  225.4 8.2 %copy-start.14 = (bf16[256,64]{0,1:T(8,128)(2,1)S(1)}, bf16[256,64]{0,1:T(8,128)(2,1)}, u32[]{:S(2)}) copy-start(bf16[256,64]{0,1:T(8,128)(2,1)} %convolution_convert_fusion) | copy-start | bytes 98308
  236.3 6.0 %copy-start.19 = (f32[4,1024]{1,0:T(4,128)S(1)}, f32[4,1024]{1,0:T(4,128)}, u32[]{:S(2)}) copy-start(f32[4,1024]{1,0:T(4,128)} %mul.342) | copy-start | bytes 49156
  260.3 4.8 copy-start.6
  260.3 4.8 copy-start.18
  260.9 4.2 copy-start.4
  261.0 4.2 copy-start.5
  265.2 6.4 %copy-start.15 = (bf16[256,64]{0,1:T(8,128)(2,1)S(1)}, bf16[256,64]{0,1:T(8,128)(2,1)}, u32[]{:S(2)}) copy-start(bf16[256,64]{0,1:T(8,128)(2,1)} %convolution_convert_fusion) | copy-start | bytes 98308
  276.2 200.8 %all-gather.12.cloned.1.call-start = ((), (), s32[]{:S(2)}) async-start(), calls=%async_computation.2 | async-start | bytes 9437184 | tf_op jit(solution)/shard_map/all_gather | solution.py:36
  276.3 7.1 %copy-start.24 = (f32[64]{0:T(128)S(1)}, f32[64]{0:T(128)}, u32[]{:S(2)}) copy-start(f32[64]{0:T(128)} %copy-done.23) | copy-start | bytes 772
  289.9 5.7 copy-start.21
  479.5 62.9 %copy-start.20 = (f32[64]{0:T(128)S(1)}, f32[64]{0:T(128)}, u32[]{:S(2)}) copy-start(f32[64]{0:T(128)} %get-tuple-element.343) | copy-start | bytes 772
Sparse Core Ops, SparseCore 0:
  25.9 87.3 all-gather.9
  116.4 80.5 all-gather.7
  276.3 150.7 all-reduce.2
  429.2 47.7 all-gather.11
where the time goes:
time: 576 us; the launch traced here: 570 us
  waiting for transfers between devices  225 us (39%)
  local copies, waits for them, and re-layouts  132 us (23%)
  other arithmetic  127 us (22%)
  matrix products  49.5 us (9%)
  blocking collectives  20.2 us (4%)
  between operations  15.8 us (3%)
    psum x1, waiting for transfers between devices, on_device(): down_total, up_total = lax.psum((down_portion, up_portion), ('dp', 'ctx'))  116 us
    all_gather x1, waiting for transfers between devices, entering(): pieces = jax.tree.map(lambda part: lax.all_gather(part, axis), value)  67.2 us
    select_n x7, other arithmetic, lap(): jnp.where(position < mine, new, old)  43 us
    all_gather x1, waiting for transfers between devices, carried_in(): lax.all_gather(a.astype(kind), axis)  41.6 us
    add x7, other arithmetic, combine(): earlier[1] * later[0][:, None, None] + later[1]  32.7 us
    dynamic_slice x14, local copies, waits for them, and re-layouts, lap(): longer = join(running, jax.tree.map(lambda part: part[position], pieces))  32.2 us
    dynamic_slice x14, local copies, waits for them, and re-layouts, one(): lax.dynamic_index_in_dim(a, source, 0, False).astype(own.dtype)  30 us
    unnamed x58, local copies, waits for them, and re-layouts  19.1 us
  transfers between devices with their start and end apart: 4, of which 3 were waited for; matrix products, arithmetic and copies ran while one was open for 27% of the time, Pallas kernels for 0%

commit v1 on v0

--- a/solution.py
+++ b/solution.py
@@ -190,7 +190,7 @@
         row_count, H, P_SIZE
     ) + skip_coefficients[None, :, None] * d_ssd.reshape(row_count, H, P_SIZE)
     input_gradient = grad_heads.reshape(row_count, INNER_CHANNELS).astype(jnp.bfloat16)
-    down_total, up_total = lax.psum((down_portion, up_portion), ("dp", "ctx"))
+    down_total, up_total = lax.psum(lax.psum((down_portion, up_portion), "ctx"), "dp")
     down_root_mean = jnp.sqrt(jnp.mean(down_total * down_total) + CLIP_EPSILON)
     up_root_mean = jnp.sqrt(jnp.mean(up_total * up_total) + CLIP_EPSILON)
     device_total = lax.axis_size(("dp", "ctx"))

time: 576 us -> 583 us (1.012)
  waiting for transfers between devices: 225 us -> 233 us
    psum x1 -> x2, waiting for transfers between devices: 116 us -> 122 us  [the longest x1 64.7 us: on_device(): lax.psum((down_portion, up_portion), 'ctx')]
  transfers between devices with their start and end apart: 4 -> 5, of which waited for: 3 -> 4; matrix products, arithmetic and copies ran while one was open for 27% -> 26% of each run, Pallas kernels for 0% -> 0%
where the time goes in v1:
time: 583 us; the launch traced here: 578 us
  waiting for transfers between devices  233 us (40%)
  local copies, waits for them, and re-layouts  132 us (23%)
  other arithmetic  128 us (22%)
  matrix products  49.4 us (8%)
  blocking collectives  19.3 us (3%)
  between operations  15.9 us (3%)
    all_gather x1, waiting for transfers between devices, entering(): pieces = jax.tree.map(lambda part: lax.all_gather(part, axis), value)  67.3 us
    psum x1, waiting for transfers between devices, on_device(): lax.psum((down_portion, up_portion), 'ctx')  64.7 us
    psum x1, waiting for transfers between devices, on_device(): lax.psum(lax.psum((down_portion, up_portion), 'ctx'), 'dp')  57.6 us
    all_gather x1, waiting for transfers between devices, carried_in(): lax.all_gather(a.astype(kind), axis)  42.9 us
    select_n x7, other arithmetic, lap(): jnp.where(position < mine, new, old)  42.9 us
    add x7, other arithmetic, combine(): earlier[1] * later[0][:, None, None] + later[1]  32.8 us
    dynamic_slice x14, local copies, waits for them, and re-layouts, lap(): longer = join(running, jax.tree.map(lambda part: part[position], pieces))  32.3 us
    dynamic_slice x14, local copies, waits for them, and re-layouts, one(): lax.dynamic_index_in_dim(a, source, 0, False).astype(own.dtype)  30 us
  transfers between devices with their start and end apart: 5, of which 4 were waited for; matrix products, arithmetic and copies ran while one was open for 26% of the time, Pallas kernels for 0%

profile of v1, /device:TPU:0, one launch (start us, length us, event | category | flops | bytes accessed | tf_op | source)
XLA Modules:
  0.0 577.6 jit_solution(285175758854780803)
XLA Ops:
  14.9 3.0 copy.131
  17.9 3.8 fusion.3
  28.2 5.7 fusion.1
  33.9 11.1 %all-gather = f32[8,1,64]{2,1,0:T(1,128)} all-gather(f32[1,1,64]{2,1,0:T(1,128)S(1)} %copy-done.22), channel_id=2, replica_groups=mesh['dp'=16,'ctx'=8] {'ctx'}, dimensions={0}, use_global_device_ids=true | all-gather | bytes 2304 | tf_op jit(solution)/shard_map/all_gather | solution.py:19
  46.1 67.3 %all-gather.10.cloned.1.call-done = f32[512,128,64]{1,2,0:T(8,128)} async-done(((f32[64,128,64]{1,2,0:T(8,128)}), f32[512,128,64]{1,2,0:T(8,128)}) %all-gather.10.cloned.1.call-update) | async-done | bytes 16777232 | tf_op jit(solution)/shard_map/all_gather | solution.py:19
  113.4 80.0 %while.19 = (s32[]{:T(128)}, f32[64,128,64]{2,1,0:T(8,128)}, s32[]{:T(128)}, f32[8,64]{1,0:T(8,128)}, f32[8,64,128,64]{2,3,1,0:T(8,128)}, /*index=5*/s32[]{:T(128)}, s32[]{:T(128)}) while((s32[]{:T(128)}, f32[64,128,64]{2,1,0:T(8,128)}, s32[]{:T(128)}, f32[8,64]{1,0:T(8,128)}, f32[8,64,128,64]{2,3,1,0:T(8,128)}, ...), condition=%wide.region_3.4_spmd.clone, body=%wide.region_2.3_spmd.clone.sunk | while | flops 2097156 | bytes 14680945 | solution.py:28
  115.1 2.8 copy.195
  118.6 4.8 fusion.43
  125.2 2.8 copy.195
  128.7 6.1 %fusion.43 = f32[64,128,64]{2,1,0:T(8,128)} fusion(f32[1,64,128,64]{3,2,1,0:T(8,128)} %copy.195, f32[64,128,64]{2,1,0:T(8,128)} %get-tuple-element.420, f32[64]{0:T(128)S(1)} %dynamic-slice_bitcast_fusion.2, pred[]{:T(512)S(6)} %compare.3, pred[]{:T(512)S(6)} %lt.51), kind=kLoop, calls=%fused_computation.4.clone.1 | loop fusion | flops 2097152 | bytes 6291714 | tf_op jit(solution)/shard_map/while/body/eval_jaxpr/jit(_where)/select_n | solution.py:26
  136.5 2.8 copy.195
  140.0 6.1 %fusion.43 = f32[64,128,64]{2,1,0:T(8,128)} fusion(f32[1,64,128,64]{3,2,1,0:T(8,128)} %copy.195, f32[64,128,64]{2,1,0:T(8,128)} %get-tuple-element.420, f32[64]{0:T(128)S(1)} %dynamic-slice_bitcast_fusion.2, pred[]{:T(512)S(6)} %compare.3, pred[]{:T(512)S(6)} %lt.51), kind=kLoop, calls=%fused_computation.4.clone.1 | loop fusion | flops 2097152 | bytes 6291714 | tf_op jit(solution)/shard_map/while/body/eval_jaxpr/jit(_where)/select_n | solution.py:26
  147.8 2.8 copy.195
  151.3 6.3 %fusion.43 = f32[64,128,64]{2,1,0:T(8,128)} fusion(f32[1,64,128,64]{3,2,1,0:T(8,128)} %copy.195, f32[64,128,64]{2,1,0:T(8,128)} %get-tuple-element.420, f32[64]{0:T(128)S(1)} %dynamic-slice_bitcast_fusion.2, pred[]{:T(512)S(6)} %compare.3, pred[]{:T(512)S(6)} %lt.51), kind=kLoop, calls=%fused_computation.4.clone.1 | loop fusion | flops 2097152 | bytes 6291714 | tf_op jit(solution)/shard_map/while/body/eval_jaxpr/jit(_where)/select_n | solution.py:26
  159.4 2.8 copy.195
  162.9 6.1 %fusion.43 = f32[64,128,64]{2,1,0:T(8,128)} fusion(f32[1,64,128,64]{3,2,1,0:T(8,128)} %copy.195, f32[64,128,64]{2,1,0:T(8,128)} %get-tuple-element.420, f32[64]{0:T(128)S(1)} %dynamic-slice_bitcast_fusion.2, pred[]{:T(512)S(6)} %compare.3, pred[]{:T(512)S(6)} %lt.51), kind=kLoop, calls=%fused_computation.4.clone.1 | loop fusion | flops 2097152 | bytes 6291714 | tf_op jit(solution)/shard_map/while/body/eval_jaxpr/jit(_where)/select_n | solution.py:26
  169.0 2.4 constant_dynamic-slice_fusion.5
  171.3 2.8 copy.195
  174.8 6.8 %fusion.43 = f32[64,128,64]{2,1,0:T(8,128)} fusion(f32[1,64,128,64]{3,2,1,0:T(8,128)} %copy.195, f32[64,128,64]{2,1,0:T(8,128)} %get-tuple-element.420, f32[64]{0:T(128)S(1)} %dynamic-slice_bitcast_fusion.2, pred[]{:T(512)S(6)} %compare.3, pred[]{:T(512)S(6)} %lt.51), kind=kLoop, calls=%fused_computation.4.clone.1 | loop fusion | flops 2097152 | bytes 6291714 | tf_op jit(solution)/shard_map/while/body/eval_jaxpr/jit(_where)/select_n | solution.py:26
  183.3 2.8 copy.195
  186.9 6.5 %fusion.43 = f32[64,128,64]{2,1,0:T(8,128)} fusion(f32[1,64,128,64]{3,2,1,0:T(8,128)} %copy.195, f32[64,128,64]{2,1,0:T(8,128)} %get-tuple-element.420, f32[64]{0:T(128)S(1)} %dynamic-slice_bitcast_fusion.2, pred[]{:T(512)S(6)} %compare.3, pred[]{:T(512)S(6)} %lt.51), kind=kLoop, calls=%fused_computation.4.clone.1 | loop fusion | flops 2097152 | bytes 6291714 | tf_op jit(solution)/shard_map/while/body/eval_jaxpr/jit(_where)/select_n | solution.py:26
  193.4 2.9 multiply_convert_fusion.2
  196.3 2.9 fusion.15
  199.2 8.2 %fusion.8 = f32[1,256,64,64]{1,3,2,0:T(8,128)} fusion(f32[4,16,64,256]{3,2,1,0:T(8,128)} %fusion.15, bf16[64,256,256]{2,1,0:T(8,128)(2,1)S(1)} %copy-done.1, f32[256,64]{0,1:T(8,128)S(1)} %copy.139, f32[256,64,64]{0,2,1:T(8,128)} %bitcast.133, f32[256,64]{0,1:T(8,128)S(1)} %get-tuple-element.340), kind=kOutput, calls=%fused_computation.22 | convolution fusion | flops 541065216 | bytes 21102592 | tf_op jit(solution)/shard_map/khij,kjhp->kihp/dot_general | solution.py:107
  207.4 5.8 copy.145
  213.2 6.3 %add_multiply_fusion = f32[256,4096]{1,0:T(8,128)} fusion(f32[256,4096]{1,0:T(8,128)} %copy.145, f32[4096]{0:T(1024)S(1)} %mul.324, bf16[256,4096]{1,0:T(8,128)(2,1)} %param.18, bf16[256,4096]{1,0:T(8,128)(2,1)S(1)} %copy-done.8), kind=kLoop, calls=%fused_computation.29 | loop fusion | flops 9437184 | bytes 12599296 | tf_op jit(solution)/shard_map/mul | solution.py:136
  219.4 6.0 %reshape.335 = f32[256,4,1024]{2,1,0:T(4,128)} reshape(f32[256,4096]{1,0:T(8,128)} %add_multiply_fusion) | data formatting | bytes 8388608 | tf_op jit(solution)/shard_map/reshape | solution.py:136
  225.4 8.2 %fusion.19 = f32[256,4096]{1,0:T(8,128)S(1)} fusion(bf16[256,2048]{1,0:T(8,128)(2,1)S(1)} %copy-done, bf16[2048,4096]{1,0:T(8,128)(2,1)} %all-gather.8.cloned.1.call-done), kind=kOutput, calls=%fused_computation.71 | convolution fusion | flops 4294967296 | bytes 22020096 | tf_op jit(solution)/shard_map/dot_general | solution.py:159
  233.6 2.7 fusion.4
  236.3 6.0 %reshape.336 = f32[256,4,1024]{2,1,0:T(4,128)} reshape(f32[256,4096]{1,0:T(8,128)} %fusion.4) | data formatting | bytes 8388608 | tf_op jit(solution)/shard_map/reshape | solution.py:162
  242.3 4.8 multiply_reduce_fusion.1
  247.8 5.8 copy.175
  254.4 5.8 %copy.174 = f32[32,8,4,1024]{3,1,2,0:T(8,128)} copy(f32[32,8,4,1024]{3,2,1,0:T(4,128)S(1)} %bitcast.143) | data formatting | bytes 8388608
  261.0 4.2 copy.173
  265.2 6.4 %fusion.18 = (bf16[256,4096]{1,0:T(8,128)(2,1)}, f32[256,4096]{1,0:T(8,128)}, bf16[256,4096]{1,0:T(8,128)(2,1)S(1)}) fusion(bf16[256,4096]{1,0:T(8,128)(2,1)} %param.18, f32[256,4096]{1,0:T(8,128)S(1)} %bitcast.137, f32[256,4096]{1,0:T(8,128)S(1)} %copy-done.4, f32[256,4096]{1,0:T(8,128)} %bitcast.138, f32[256,4096]{1,0:T(8,128)S(1)} %bitcast.139, ...), kind=kLoop, calls=%fused_computation.70 | loop fusion | flops 15728640 | bytes 31473664 | tf_op jit(solution)/shard_map/convert_element_type | solution.py:167
  273.1 3.1 convolution_multiply_fusion.2
  276.3 64.7 %all-reduce.7.cloned.1.call-done = (f32[64,4096]{1,0:T(8,128)}, f32[64,2048]{1,0:T(8,128)}) async-done(((f32[64,4096]{1,0:T(8,128)}, f32[64,2048]{1,0:T(8,128)}), (f32[64,4096]{1,0:T(8,128)}, f32[64,2048]{1,0:T(8,128)})) %all-reduce.7.cloned.1.call-update) | async-done | bytes 1572880 | tf_op jit(solution)/shard_map/psum | solution.py:193
  341.1 3.8 fusion.2
  344.9 3.3 copy.151
  348.2 4.1 add_convert_fusion.1
  352.3 2.3 mul.307
  354.6 5.6 copy.156
  360.2 8.2 %all-gather.3 = bf16[8,1,64]{2,1,0:T(2,128)(2,1)S(1)} all-gather(bf16[1,1,64]{2,1,0:T(2,128)(2,1)S(1)} %copy-done.21), channel_id=5, replica_groups=mesh['dp'=16,'ctx'=8] {'ctx'}, dimensions={0}, use_global_device_ids=true | all-gather | bytes 1152 | tf_op jit(solution)/shard_map/all_gather | solution.py:36
  368.4 6.9 %fusion.20 = f32[64,64,256]{2,1,0:T(8,128)} fusion(bf16[256,64,64]{0,2,1:T(8,128)(2,1)S(1)} %bitcast.136, bf16[64,256,256]{2,1,0:T(8,128)(2,1)} %fusion.1), kind=kOutput, calls=%fused_computation.72 | convolution fusion | flops 536870912 | bytes 14680064 | tf_op jit(solution)/shard_map/khij,kihp->kjhp/dot_general | solution.py:168
  375.3 57.6 %all-reduce.5.cloned.1.call-done = (f32[64,4096]{1,0:T(8,128)}, f32[64,2048]{1,0:T(8,128)}) async-done(((f32[64,4096]{1,0:T(8,128)}, f32[64,2048]{1,0:T(8,128)}), (f32[64,4096]{1,0:T(8,128)}, f32[64,2048]{1,0:T(8,128)})) %all-reduce.5.cloned.1.call-update) | async-done | bytes 1572880 | tf_op jit(solution)/shard_map/psum | solution.py:193
  441.2 42.9 %all-gather.12.cloned.1.call-done = bf16[512,128,64]{1,2,0:T(8,128)(2,1)} async-done(((bf16[64,128,64]{1,2,0:T(8,128)(2,1)}), bf16[512,128,64]{1,2,0:T(8,128)(2,1)}) %all-gather.12.cloned.1.call-update) | async-done | bytes 8388624 | tf_op jit(solution)/shard_map/all_gather | solution.py:36
  484.1 2.5 broadcast_in_dim.45
  486.7 62.9 %while.18 = (s32[]{:T(128)}, f32[64,128,64]{2,1,0:T(8,128)}, s32[]{:T(128)}, bf16[8,64]{1,0:T(8,128)(2,1)S(1)}, bf16[8,64,128,64]{2,3,1,0:T(8,128)(2,1)}, /*index=5*/s32[]{:T(128)}, s32[]{:T(128)}, s32[]{:T(128)}, s32[]{:T(128)}) while((s32[]{:T(128)}, f32[64,128,64]{2,1,0:T(8,128)}, s32[]{:T(128)}, bf16[8,64]{1,0:T(8,128)(2,1)S(1)}, ...), condition=%wide.region_7.8_spmd, body=%wide.region_6.7_spmd.sunk | while | flops 1572934 | bytes 9437979 | solution.py:51
  486.7 2.3 constant_dynamic-slice_fusion.4
  491.0 4.7 convert_add_fusion.2
  495.7 2.3 constant_dynamic-slice_fusion.4
  500.0 4.7 convert_add_fusion.2
  504.7 2.3 constant_dynamic-slice_fusion.4
  509.0 4.7 convert_add_fusion.2
  513.7 2.3 constant_dynamic-slice_fusion.4
  518.0 4.7 convert_add_fusion.2
  522.7 2.3 constant_dynamic-slice_fusion.4
  527.0 4.7 convert_add_fusion.2
  531.6 2.3 constant_dynamic-slice_fusion.4
  536.0 4.7 convert_add_fusion.2
  545.0 4.7 convert_add_fusion.2
  549.6 8.3 %convolution_add_fusion = f32[64,64,256]{2,1,0:T(8,128)} fusion(f32[64,64,256]{2,1,0:T(8,128)} %fusion.20, bf16[256,64,128]{2,0,1:T(8,128)(2,1)} %copy-done.2, f32[64,128,64]{2,1,0:T(8,128)} %get-tuple-element.212, f32[64]{0:T(128)S(1)} %copy-done.20), kind=kOutput, calls=%fused_computation.33 | convolution fusion | flops 270532608 | bytes 14680320 | tf_op jit(solution)/shard_map/kjhn,khnp->kjhp/dot_general | solution.py:186
  558.0 5.6 copy.157
  563.6 7.3 %add_convert_fusion = bf16[256,4096]{1,0:T(8,128)(2,1)} fusion(f32[256,4096]{1,0:T(8,128)} %get-tuple-element.336, f32[256,4096]{1,0:T(8,128)} %copy.156, f32[256,4096]{1,0:T(8,128)} %copy.157, f32[4096]{0:T(1024)S(1)} %mul.324), kind=kLoop, calls=%fused_computation.24 | loop fusion | flops 4194304 | bytes 14696448 | tf_op jit(solution)/shard_map/convert_element_type | solution.py:192
  (138 shorter events, 57.5 us)
Async XLA Ops:
  7.2 37.9 %copy-start = (bf16[256,2048]{1,0:T(8,128)(2,1)S(1)}, bf16[256,2048]{1,0:T(8,128)(2,1)}, u32[]{:S(2)}) copy-start(bf16[256,2048]{1,0:T(8,128)(2,1)} %param.29) | copy-start | bytes 3145732
  7.2 7.7 %copy-start.7 = (bf16[256,4096]{1,0:T(8,128)(2,1)S(1)}, bf16[256,4096]{1,0:T(8,128)(2,1)}, u32[]{:S(2)}) copy-start(bf16[256,4096]{1,0:T(8,128)(2,1)} %param.17) | copy-start | bytes 6291460
  7.2 106.2 %all-gather.10.cloned.1.call-start = ((), (), s32[]{:S(2)}) async-start(), calls=%async_computation.1 | async-start | bytes 18874368 | tf_op jit(solution)/shard_map/all_gather | solution.py:19
  10.7 0.6 copy-start.12
  12.0 9.7 %copy-start.23 = (f32[64]{0:T(128)}, f32[64]{0:T(128)S(1)}, u32[]{:S(2)}) copy-start(f32[64]{0:T(128)S(1)} %get-tuple-element.346) | copy-start | bytes 772
  17.9 5.8 %copy-start.3 = (f32[256,4096]{0,1:T(8,128)S(1)}, f32[256,4096]{0,1:T(8,128)}, u32[]{:S(2)}) copy-start(f32[256,4096]{0,1:T(8,128)} %copy.131) | copy-start | bytes 12582916
  21.7 1.9 copy-start.2
  23.6 3.1 copy-start.11
  23.6 3.3 copy-start.13
  23.6 3.4 copy-start.25
  23.6 3.6 copy-start.17
  23.7 4.2 copy-start.10
  25.9 199.5 %all-gather.8.cloned.1.call-start = ((), (), s32[]{:S(2)}) async-start(), calls=%async_computation | async-start | bytes 16908288 | tf_op jit(solution)/shard_map/all_gather | solution.py:158
  26.7 314.3 %all-reduce.7.cloned.1.call-start = ((), (), s32[]{:S(2)}) async-start(), calls=%async_computation.4 | async-start | bytes 3145728 | tf_op jit(solution)/shard_map/psum | solution.py:193
  28.2 5.7 copy-start.22
  28.2 16.8 %copy-start.16 = (bf16[64,2048]{1,0:T(8,128)(2,1)S(1)}, bf16[64,2048]{1,0:T(8,128)(2,1)}, u32[]{:S(2)}) copy-start(bf16[64,2048]{1,0:T(8,128)(2,1)} %param.27) | copy-start | bytes 786436
  193.4 5.8 %copy-start.1 = (bf16[64,256,256]{2,1,0:T(8,128)(2,1)S(1)}, bf16[64,256,256]{2,1,0:T(8,128)(2,1)}, u32[]{:S(2)}) copy-start(bf16[64,256,256]{2,1,0:T(8,128)(2,1)} %fusion.1) | copy-start | bytes 25165828
  207.4 5.8 copy-start.8
  225.4 8.2 %copy-start.9 = (bf16[64,4096]{1,0:T(8,128)(2,1)S(1)}, bf16[64,4096]{1,0:T(8,128)(2,1)}, u32[]{:S(2)}) copy-start(bf16[64,4096]{1,0:T(8,128)(2,1)} %param.26) | copy-start | bytes 1572868
  225.4 8.2 %copy-start.14 = (bf16[256,64]{0,1:T(8,128)(2,1)S(1)}, bf16[256,64]{0,1:T(8,128)(2,1)}, u32[]{:S(2)}) copy-start(bf16[256,64]{0,1:T(8,128)(2,1)} %convolution_convert_fusion) | copy-start | bytes 98308
  236.3 6.0 %copy-start.19 = (f32[4,1024]{1,0:T(4,128)S(1)}, f32[4,1024]{1,0:T(4,128)}, u32[]{:S(2)}) copy-start(f32[4,1024]{1,0:T(4,128)} %mul.342) | copy-start | bytes 49156
  260.3 4.8 copy-start.6
  260.3 4.8 copy-start.18
  261.0 4.2 copy-start.4
  261.0 4.2 copy-start.5
  265.2 6.4 %copy-start.15 = (bf16[256,64]{0,1:T(8,128)(2,1)S(1)}, bf16[256,64]{0,1:T(8,128)(2,1)}, u32[]{:S(2)}) copy-start(bf16[256,64]{0,1:T(8,128)(2,1)} %convolution_convert_fusion) | copy-start | bytes 98308
  276.2 156.7 %all-reduce.5.cloned.1.call-start = ((), (), s32[]{:S(2)}) async-start(), calls=%async_computation.3 | async-start | bytes 3145728 | tf_op jit(solution)/shard_map/psum | solution.py:193
  341.0 143.2 %all-gather.12.cloned.1.call-start = ((), (), s32[]{:S(2)}) async-start(), calls=%async_computation.2 | async-start | bytes 9437184 | tf_op jit(solution)/shard_map/all_gather | solution.py:36
  341.1 7.1 %copy-start.24 = (f32[64]{0:T(128)S(1)}, f32[64]{0:T(128)}, u32[]{:S(2)}) copy-start(f32[64]{0:T(128)} %copy-done.23) | copy-start | bytes 772
  354.6 5.6 copy-start.21
  486.7 63.0 %copy-start.20 = (f32[64]{0:T(128)S(1)}, f32[64]{0:T(128)}, u32[]{:S(2)}) copy-start(f32[64]{0:T(128)} %get-tuple-element.345) | copy-start | bytes 772
Sparse Core Ops, SparseCore 0:
  26.0 87.3 all-gather.9
  116.6 80.5 all-gather.7
  276.3 64.5 all-reduce.6
  344.2 88.6 all-reduce.4
  435.1 49.0 all-gather.11
